TPU v7x, 128 devices: a whole 4x4x4 slice. The times are simulated.
128 devices in a mesh: replica: 4 (over z), shard: 16 (over y, x_lo, core), tensor: 2 (over x_hi).
Axes of the slice: x: 4 (x_hi: 2, x_lo: 2; x = x_hi * 2 + x_lo), y: 4, z: 4, core: 2. Of those that a mesh axis runs over, the one named last changes fastest.
Arguments:
- trained_up: bfloat16 [4, 1024, 4096], P('replica', None, 'tensor'), may hold values from -6 to 6
- trained_down: bfloat16 [4, 4096, 1024], P('replica', 'tensor'), may hold values from -6 to 6
- trained_embed: bfloat16 [4, 32768, 1024], P('replica', ('shard', 'tensor')), may hold values from -6 to 6
- trained_norm: bfloat16 [4, 2, 1024], P('replica'), may hold values from 0.099609375 to 1.8984375
- master_up: float32 [1024, 4096], P(('replica', 'shard', 'tensor')), may hold values from -6 to 6
- moment_up: float32 [1024, 4096], P(('replica', 'shard', 'tensor')), may hold values from -4 to 4
- master_down: float32 [2, 2048, 1024], P('tensor', ('replica', 'shard')), may hold values from -6 to 6
- moment_down: float32 [2, 2048, 1024], P('tensor', ('replica', 'shard')), may hold values from -4 to 4
- master_embed: float32 [32, 1024, 1024], P(('shard', 'tensor'), 'replica'), may hold values from -6 to 6
- moment_embed: float32 [32, 1024, 64], P(('shard', 'tensor'), 'replica'), may hold values from -4 to 4
- master_norm: float32 [2, 1024], replicated, may hold values from 0.1 to 1.9
- moment_norm: float32 [2, 1024], replicated, may hold values from -2 to 2
- embed_basis: float32 [1024, 64], replicated, may hold values from -0.1875 to 0.1875
Outputs:
- recast_up: bfloat16 [1024, 4096], P(None, 'tensor')
- recast_down: bfloat16 [4096, 1024], P('tensor')
- recast_embed: bfloat16 [32768, 1024], P(('shard', 'tensor'))
- recast_norm: bfloat16 [2, 1024], replicated
- stored_up: float32 [1024, 4096], P(('replica', 'shard', 'tensor'))
- velocity_up: float32 [1024, 4096], P(('replica', 'shard', 'tensor'))
- stored_down: float32 [2, 2048, 1024], P('tensor', ('replica', 'shard'))
- velocity_down: float32 [2, 2048, 1024], P('tensor', ('replica', 'shard'))
- stored_embed: float32 [32, 1024, 1024], P(('shard', 'tensor'), 'replica')
- velocity_embed: float32 [32, 1024, 64], P(('shard', 'tensor'), 'replica')
- stored_norm: float32 [2, 1024], replicated
- velocity_norm: float32 [2, 1024], replicated
All inputs are finite; a program needn't handle non-finite values.
Results may differ from a plain program's by a relative error of at most 0.012.
Values may be sent and summed in bfloat16 or wider, within the bound.
A program may use at most 128 MiB of HBM per device.

v0:
```python
import jax
import jax.numpy as jnp
from jax import lax
from jax.sharding import PartitionSpec as P


def outer_step(master, moment, summed, groups):
    difference = master - summed / groups
    velocity = 0.5 * moment + difference
    return (master - 0.7 * (difference + 0.5 * velocity), velocity)


def body(
    trained_up,
    trained_down,
    trained_embed,
    trained_norm,
    master_up,
    moment_up,
    master_down,
    moment_down,
    master_embed,
    moment_embed,
    master_norm,
    moment_norm,
    embed_basis,
):
    replicas = lax.axis_size("replica")
    shards = lax.axis_size("shard")
    tensors = lax.axis_size("tensor")
    shard_pos = lax.axis_index("shard")
    width = embed_basis.shape[0]
    rows_up = master_up.shape[0]
    half_cols = trained_up.shape[2]
    rows_down = master_down.shape[1]
    up_blocks = trained_up[0].reshape(replicas, shards, tensors, rows_up, half_cols)
    up_own = lax.dynamic_index_in_dim(up_blocks, shard_pos, 1, keepdims=False)
    down_blocks = trained_down[0].reshape(replicas, shards, rows_down, width)
    down_own = lax.dynamic_index_in_dim(down_blocks, shard_pos, 1, keepdims=False)
    up_summed, down_summed = (
        lax.psum_scatter(
            up_own.astype(jnp.float32).astype(jnp.bfloat16),
            "replica",
            scatter_dimension=0,
            tiled=True,
        ).astype(jnp.float32),
        lax.psum_scatter(
            down_own.astype(jnp.float32).astype(jnp.bfloat16),
            "replica",
            scatter_dimension=0,
            tiled=True,
        ).astype(jnp.float32),
    )
    up_summed = lax.all_to_all(up_summed, "tensor", split_axis=1, concat_axis=3, tiled=True)
    stored_up, velocity_up = outer_step(
        master_up, moment_up, up_summed.reshape(rows_up, half_cols * tensors), replicas
    )
    stored_down, velocity_down = outer_step(master_down, moment_down, down_summed, replicas)
    norm_summed = lax.psum(trained_norm[0].astype(jnp.float32), "replica")
    stored_norm, velocity_norm = outer_step(master_norm, moment_norm, norm_summed, replicas)
    embed_own = master_embed[0]
    rows_embed = embed_own.shape[0]
    embed_terms = trained_embed[0].reshape(replicas, rows_embed, width).astype(jnp.float32)
    embed_summed = lax.psum_scatter(
        embed_terms.astype(jnp.bfloat16), "replica", scatter_dimension=0, tiled=True
    ).astype(jnp.float32)[0]
    coefficient = jnp.dot(
        embed_own - embed_summed / replicas, embed_basis, precision=lax.Precision.HIGHEST
    )
    velocity_rows = 0.5 * moment_embed[0] + coefficient
    stored_rows = embed_own - 0.7 * jnp.dot(
        coefficient + 0.5 * velocity_rows, embed_basis.T, precision=lax.Precision.HIGHEST
    )
    up_piece = lax.all_to_all(
        stored_up.astype(jnp.bfloat16), "tensor", split_axis=1, concat_axis=0, tiled=True
    )
    down_piece = stored_down[0].astype(jnp.bfloat16)
    recast_up, recast_down = (
        lax.all_gather(up_piece, ("replica", "shard"), axis=0, tiled=True),
        lax.all_gather(down_piece, ("replica", "shard"), axis=0, tiled=True),
    )
    recast_embed = lax.all_gather(stored_rows.astype(jnp.bfloat16), "replica", axis=0, tiled=True)
    return (
        recast_up,
        recast_down,
        recast_embed,
        stored_norm.astype(jnp.bfloat16),
        stored_up,
        velocity_up,
        stored_down,
        velocity_down,
        stored_rows[None],
        velocity_rows[None],
        stored_norm,
        velocity_norm,
    )


def solution(mesh):
    in_specs = (
        P("replica", None, "tensor"),
        P("replica", "tensor", None),
        P("replica", ("shard", "tensor"), None),
        P("replica", None, None),
        P(("replica", "shard", "tensor"), None),
        P(("replica", "shard", "tensor"), None),
        P("tensor", ("replica", "shard"), None),
        P("tensor", ("replica", "shard"), None),
        P(("shard", "tensor"), "replica", None),
        P(("shard", "tensor"), "replica", None),
        P(),
        P(),
        P(),
    )
    out_specs = (
        P(None, "tensor"),
        P("tensor", None),
        P(("shard", "tensor"), None),
        P(),
        P(("replica", "shard", "tensor"), None),
        P(("replica", "shard", "tensor"), None),
        P("tensor", ("replica", "shard"), None),
        P("tensor", ("replica", "shard"), None),
        P(("shard", "tensor"), "replica", None),
        P(("shard", "tensor"), "replica", None),
        P(),
        P(),
    )
    return jax.shard_map(body, mesh=mesh, in_specs=in_specs, out_specs=out_specs, check_vma=False)
```

profile of v0, /device:TPU:1, one launch (start us, length us, event | category | flops | bytes accessed | tf_op | source)
XLA Modules:
  0.0 376.6 jit_solution(8853071086595991756)
XLA Ops:
  7.2 0.0 copy-start
  7.2 0.0 copy-start.1
  7.2 0.0 copy-start.4
  7.2 0.0 reduce-scatter.6.cloned.1.call-start
  7.3 0.0 copy-start.12
  7.3 0.7 reduce-scatter.6.cloned.1.call-update
  7.9 0.0 copy-start.7
  8.0 0.0 copy-start.8
  8.0 0.0 all-reduce.3.cloned.1.call-start
  8.0 1.7 copy_bitcast_fusion
  9.7 0.0 all-reduce.3.cloned.1.call-update
  9.7 0.0 reduce-scatter.4.cloned.1.call-start
  9.8 0.0 copy-start.11
  9.8 1.7 dynamic-slice_bitcast_fusion
  11.5 0.0 reduce-scatter.4.cloned.1.call-update
  11.5 0.0 all-gather.7.cloned.1.call-start
  11.6 32.1 %reduce-scatter.6.cloned.1.call-done = bf16[1,256,1024]{2,1,0:T(8,128)(2,1)} async-done(((bf16[4,256,1024]{2,1,0:T(8,128)(2,1)}), bf16[1,256,1024]{2,1,0:T(8,128)(2,1)}) %reduce-scatter.6.cloned.1.call-update) | async-done | bytes 524304 | tf_op jit(solution)/shard_map/reduce_scatter | solution.py:64
  43.6 0.0 copy-done
  43.6 0.0 copy-done.1
  43.6 2.2 fusion.1
  45.8 0.0 copy-done.4
  45.8 2.2 fusion.16
  48.0 0.0 all-gather.7.cloned.1.call-update
  48.1 0.0 all-gather.5.cloned.1.call-start
  48.1 0.0 copy-done.12
  48.1 0.6 dynamic-slice
  48.7 37.3 %all-reduce.3.cloned.1.call-done = bf16[4,2,8,2048]{3,2,0,1:T(8,128)(2,1)} async-done(((bf16[4,2,8,2048]{3,2,0,1:T(8,128)(2,1)}), bf16[4,2,8,2048]{3,2,0,1:T(8,128)(2,1)}) %all-reduce.3.cloned.1.call-update) | async-done | bytes 262160
  86.0 1.5 dynamic-slice_convert_fusion
  87.5 8.6 %all_to_all.28 = f32[1,2,8,2048]{3,2,0,1:T(8,128)S(1)} all-to-all(f32[1,2,8,2048]{3,2,0,1:T(8,128)S(1)} %dynamic-slice_convert_fusion), channel_id=1, replica_groups=mesh['replica'=4,'shard'=16,'tensor'=2] {'tensor'}, dimensions={1} | all-to-all | bytes 262144 | tf_op jit(solution)/shard_map/all_to_all | solution.py:54
  96.1 0.7 fusion.15
  96.9 7.5 %all_to_all.29 = bf16[8,2,2048]{2,0,1:T(8,128)(2,1)} all-to-all(bf16[8,2,2048]{2,0,1:T(8,128)(2,1)S(1)} %bitcast.53), channel_id=1, replica_groups=mesh['replica'=4,'shard'=16,'tensor'=2] {'tensor'}, dimensions={1} | all-to-all | bytes 131072 | tf_op jit(solution)/shard_map/all_to_all | solution.py:74
  104.4 0.0 all-gather.5.cloned.1.call-update
  104.4 0.0 all-gather.9.cloned.1.call-start
  104.4 5.8 %reduce-scatter.4.cloned.1.call-done = bf16[1,32,1024]{2,1,0:T(8,128)(2,1)} async-done(((bf16[4,32,1024]{2,1,0:T(8,128)(2,1)}), bf16[1,32,1024]{2,1,0:T(8,128)(2,1)}) %reduce-scatter.4.cloned.1.call-update) | async-done | bytes 65552 | tf_op jit(solution)/shard_map/reduce_scatter | solution.py:47
  110.3 0.0 copy-done.6
  110.3 1.6 fusion.14
  111.9 0.0 all-gather.9.cloned.1.call-update
  111.9 6.9 %psum.7 = f32[2,1024]{1,0:T(2,128)S(1)} all-reduce(f32[2,1024]{1,0:T(2,128)S(1)} %bitcast_convert_fusion), channel_id=1, replica_groups=mesh['replica'=4,'shard'=16,'tensor'=2] {'replica'}, use_global_device_ids=true, to_apply=%region_3.4 | all-reduce | flops 2048 | bytes 16384 | tf_op jit(solution)/shard_map/psum | solution.py:59
  118.9 0.6 fusion.13
  119.5 0.6 fusion.8
  120.2 25.0 %all-gather.7.cloned.1.call-done = bf16[1024,1024]{1,0:T(8,128)(2,1)} async-done(((bf16[256,1024]{1,0:T(8,128)(2,1)}), bf16[1024,1024]{1,0:T(8,128)(2,1)}) %all-gather.7.cloned.1.call-update) | async-done | bytes 2097168 | tf_op jit(solution)/shard_map/all_gather | solution.py:82
  145.2 108.0 %all-gather.5.cloned.1.call-done = bf16[1024,2048]{1,0:T(8,128)(2,1)} async-done(((bf16[16,2048]{1,0:T(8,128)(2,1)}), bf16[1024,2048]{1,0:T(8,128)(2,1)}) %all-gather.5.cloned.1.call-update) | async-done | bytes 4194320 | tf_op jit(solution)/shard_map/all_gather | solution.py:79
  253.2 107.3 %all-gather.9.cloned.1.call-done = bf16[1,2048,1024]{2,1,0:T(8,128)(2,1)} async-done(((bf16[1,32,1024]{2,1,0:T(8,128)(2,1)}), bf16[1,2048,1024]{2,1,0:T(8,128)(2,1)}) %all-gather.9.cloned.1.call-update) | async-done | bytes 4194320 | tf_op jit(solution)/shard_map/all_gather | solution.py:80
  360.4 4.9 %copy.39 = bf16[1024,2048]{1,0:T(8,128)(2,1)} copy(bf16[1024,2048]{1,0:T(8,128)(2,1)} %all-gather.5.cloned.1.call-done) | data formatting | bytes 8388608
  365.4 0.0 copy-done.2
  365.4 2.1 copy.40
  367.5 1.0 copy-done.3
  368.5 1.3 copy.41
  (14 shorter events, 0.0 us)
Async XLA Ops:
  7.2 36.5 %copy-start = (f32[1024,64]{0,1:T(8,128)S(1)}, f32[1024,64]{0,1:T(8,128)}, u32[]{:S(2)}) copy-start(f32[1024,64]{0,1:T(8,128)} %param.25) | copy-start | bytes 786436
  7.2 36.5 %copy-start.1 = (f32[1,256,1024]{2,1,0:T(8,128)S(1)}, f32[1,256,1024]{2,1,0:T(8,128)}, u32[]{:S(2)}) copy-start(f32[1,256,1024]{2,1,0:T(8,128)} %param.21) | copy-start | bytes 3145732
  7.2 38.6 %copy-start.4 = (f32[1,256,64]{1,2,0:T(8,128)S(1)}, f32[1,256,64]{1,2,0:T(8,128)}, u32[]{:S(2)}) copy-start(f32[1,256,64]{1,2,0:T(8,128)} %param.22) | copy-start | bytes 196612
  7.2 36.4 %reduce-scatter.6.cloned.1.call-start = ((), (), s32[]{:S(2)}) async-start(), calls=%async_computation.6 | async-start | bytes 2621440 | tf_op jit(solution)/shard_map/reduce_scatter | solution.py:64
  7.3 40.9 %copy-start.12 = (u32[128]{0:T(128)S(1)}, u32[128]{0:T(128)}, u32[]{:S(2)}) copy-start(u32[128]{0:T(128)} %constant.47) | copy-start | bytes 1540
  7.9 88.2 %copy-start.7 = (f32[8,4096]{1,0:T(8,128)S(1)}, f32[8,4096]{1,0:T(8,128)}, u32[]{:S(2)}) copy-start(f32[8,4096]{1,0:T(8,128)} %param.17) | copy-start | bytes 393220
  8.0 88.2 %copy-start.8 = (f32[8,4096]{1,0:T(8,128)S(1)}, f32[8,4096]{1,0:T(8,128)}, u32[]{:S(2)}) copy-start(f32[8,4096]{1,0:T(8,128)} %param.18) | copy-start | bytes 393220
  8.0 78.0 %all-reduce.3.cloned.1.call-start = ((), (), s32[]{:S(2)}) async-start(), calls=%async_computation.9 | async-start | bytes 524288
  9.7 100.6 %copy-start.5 = (f32[1,32,1024]{2,1,0:T(8,128)S(1)}, f32[1,32,1024]{2,1,0:T(8,128)}, u32[]{:S(2)}) copy-start(f32[1,32,1024]{2,1,0:T(8,128)} %param.19) | copy-start | bytes 393220
  9.7 100.6 %copy-start.6 = (f32[1,32,1024]{2,1,0:T(8,128)S(1)}, f32[1,32,1024]{2,1,0:T(8,128)}, u32[]{:S(2)}) copy-start(f32[1,32,1024]{2,1,0:T(8,128)} %param.20) | copy-start | bytes 393220
  9.7 100.6 %reduce-scatter.4.cloned.1.call-start = ((), (), s32[]{:S(2)}) async-start(), calls=%async_computation.5 | async-start | bytes 327680 | tf_op jit(solution)/shard_map/reduce_scatter | solution.py:47
  9.8 102.1 %copy-start.11 = (bf16[1,2,1024]{2,1,0:T(2,128)(2,1)S(1)}, bf16[1,2,1024]{2,1,0:T(2,128)(2,1)}, u32[]{:S(2)}) copy-start(bf16[1,2,1024]{2,1,0:T(2,128)(2,1)} %param.16) | copy-start | bytes 12292
  11.5 107.4 %copy-start.9 = (f32[2,1024]{1,0:T(2,128)S(1)}, f32[2,1024]{1,0:T(2,128)}, u32[]{:S(2)}) copy-start(f32[2,1024]{1,0:T(2,128)} %param.23) | copy-start | bytes 24580
  11.5 107.4 %copy-start.10 = (f32[2,1024]{1,0:T(2,128)S(1)}, f32[2,1024]{1,0:T(2,128)}, u32[]{:S(2)}) copy-start(f32[2,1024]{1,0:T(2,128)} %param.24) | copy-start | bytes 24580
  11.5 133.6 %all-gather.7.cloned.1.call-start = ((), (), s32[]{:S(2)}) async-start(), calls=%async_computation.7 | async-start | bytes 2621440 | tf_op jit(solution)/shard_map/all_gather | solution.py:82
  48.1 205.1 %all-gather.5.cloned.1.call-start = ((), (), s32[]{:S(2)}) async-start(), calls=%async_computation.4 | async-start | bytes 4259840 | tf_op jit(solution)/shard_map/all_gather | solution.py:79
  104.4 256.0 %all-gather.9.cloned.1.call-start = ((), (), s32[]{:S(2)}) async-start(), calls=%async_computation.8 | async-start | bytes 4259840 | tf_op jit(solution)/shard_map/all_gather | solution.py:80
  360.4 4.9 %copy-start.2 = (bf16[1,2048,1024]{2,1,0:T(8,128)(2,1)S(1)}, bf16[1,2048,1024]{2,1,0:T(8,128)(2,1)}, u32[]{:S(2)}) copy-start(bf16[1,2048,1024]{2,1,0:T(8,128)(2,1)} %all-gather.9.cloned.1.call-done) | copy-start | bytes 12582916
  365.4 3.1 copy-start.3
Sparse Core Ops, SparseCore 0:
  10.4 33.1 reduce-scatter.5
  46.7 39.3 all-reduce.2
  89.0 21.2 reduce-scatter.3
  112.5 32.6 all-gather.6
  146.9 106.2 all-gather.4
  255.4 104.9 all-gather.8
where the time goes:
time: 377 us
  waiting for transfers between devices  316 us (84%)
  blocking collectives  23 us (6%)
  between operations  14.3 us (4%)
  local copies, waits for them, and re-layouts  13.4 us (4%)
  other arithmetic  5.09 us (1%)
  matrix products  4.38 us (1%)
    all_gather x1, waiting for transfers between devices, body(): lax.all_gather(up_piece, ('replica', 'shard'), axis=0, tiled=True)  108 us
    all_gather x1, waiting for transfers between devices, body(): lax.all_gather(down_piece, ('replica', 'shard'), axis=0, tiled=True)  107 us
    unnamed x7, waiting for transfers between devices  38.1 us
    reduce_scatter x1, waiting for transfers between devices, body(): lax.psum_scatter(embed_terms.astype(jnp.bfloat16), 'replica', scatter_dim...  32.1 us
    all_gather x1, waiting for transfers between devices, body(): lax.all_gather(stored_rows.astype(jnp.bfloat16), 'replica', axis=0, tiled...  25 us
    unnamed x30, local copies, waits for them, and re-layouts  10 us
    all_to_all x1, blocking collectives, body(): lax.all_to_all(up_summed, 'tensor', split_axis=1, concat_axis=3, tiled=True)  8.59 us
  transfers between devices with their start and end apart: 6, of which 6 were waited for; matrix products, arithmetic and copies ran while one was open for 4% of the time, Pallas kernels for 0%

commit v1 on v0

--- a/solution.py
+++ b/solution.py
@@ -2,6 +2,24 @@
 import jax.numpy as jnp
 from jax import lax
 from jax.sharding import PartitionSpec as P
+
+
+def ring_gather(value, axis, dim):
+    ways, here, hop = (lax.axis_size(axis), lax.axis_index(axis), value.shape[dim])
+    lengths = [n * ways if d == dim else n for d, n in enumerate(value.shape)]
+    full = lax.dynamic_update_slice_in_dim(
+        jnp.zeros(lengths, value.dtype), value, here * hop, axis=dim
+    )
+    going_up = going_down = value
+    for far in range(1, ways // 2 + 1):
+        going_up = lax.ppermute(going_up, axis, [(d, (d + 1) % ways) for d in range(ways)])
+        full = lax.dynamic_update_slice_in_dim(full, going_up, (here - far) % ways * hop, axis=dim)
+        if 2 * far < ways:
+            going_down = lax.ppermute(going_down, axis, [(d, (d - 1) % ways) for d in range(ways)])
+            full = lax.dynamic_update_slice_in_dim(
+                full, going_down, (here + far) % ways * hop, axis=dim
+            )
+    return full
 
 
 def outer_step(master, moment, summed, groups):
@@ -79,7 +97,7 @@
         lax.all_gather(up_piece, ("replica", "shard"), axis=0, tiled=True),
         lax.all_gather(down_piece, ("replica", "shard"), axis=0, tiled=True),
     )
-    recast_embed = lax.all_gather(stored_rows.astype(jnp.bfloat16), "replica", axis=0, tiled=True)
+    recast_embed = ring_gather(stored_rows.astype(jnp.bfloat16), "replica", 0)
     return (
         recast_up,
         recast_down,

time: 377 us -> 342 us (0.907)
  waiting for transfers between devices: 316 us -> 271 us
  blocking collectives: 23 us -> 32.3 us
    all_gather x1, waiting for transfers between devices: 108 us -> 72.1 us  [body(): lax.all_gather(up_piece, ('replica', 'shard'), axis=0, tiled=True)]
    all_gather x1 -> x0, waiting for transfers between devices: 25 us -> none  [body(): lax.all_gather(stored_rows.astype(jnp.bfloat16), 'replica', axis=0, tiled...]
    ppermute x0 -> x3, waiting for transfers between devices: none -> 10.6 us  [the longest x1 10.6 us: ring_gather(): lax.ppermute(going_down, axis, [(d, (d - 1) % ways) for d in range(ways)])]
    psum x1, blocking collectives: 6.93 us -> 16.2 us  [body(): norm_summed = lax.psum(trained_norm[0].astype(jnp.float32), 'replica')]
    unnamed x7 -> x6, waiting for transfers between devices: 38.1 us -> 42.5 us
    unnamed x30 -> x27, local copies, waits for them, and re-layouts: 10 us -> 7.6 us
  transfers between devices with their start and end apart: 6 -> 8, of which waited for: 6 -> 6; matrix products, arithmetic and copies ran while one was open for 4% -> 4% of each run, Pallas kernels for 0% -> 0%
where the time goes in v1:
time: 342 us; the launch traced here: 341 us
  waiting for transfers between devices  271 us (79%)
  blocking collectives  32.3 us (9%)
  between operations  14 us (4%)
  local copies, waits for them, and re-layouts  12.4 us (4%)
  other arithmetic  5.79 us (2%)
  matrix products  4.39 us (1%)
    all_gather x1, waiting for transfers between devices, body(): lax.all_gather(down_piece, ('replica', 'shard'), axis=0, tiled=True)  107 us
    all_gather x1, waiting for transfers between devices, body(): lax.all_gather(up_piece, ('replica', 'shard'), axis=0, tiled=True)  72.1 us
    unnamed x6, waiting for transfers between devices  42.5 us
    reduce_scatter x1, waiting for transfers between devices, body(): lax.psum_scatter(embed_terms.astype(jnp.bfloat16), 'replica', scatter_dim...  32.4 us
    psum x1, blocking collectives, body(): norm_summed = lax.psum(trained_norm[0].astype(jnp.float32), 'replica')  16.2 us
    ppermute x1, waiting for transfers between devices, ring_gather(): lax.ppermute(going_down, axis, [(d, (d - 1) % ways) for d in range(ways)])  10.6 us
    all_to_all x1, blocking collectives, body(): lax.all_to_all(up_summed, 'tensor', split_axis=1, concat_axis=3, tiled=True)  8.59 us
    unnamed x27, local copies, waits for them, and re-layouts  7.6 us
  transfers between devices with their start and end apart: 8, of which 6 were waited for; matrix products, arithmetic and copies ran while one was open for 4% of the time, Pallas kernels for 0%

profile of v1, /device:TPU:1, one launch (start us, length us, event | category | flops | bytes accessed | tf_op | source)
XLA Modules:
  0.0 341.3 jit_solution(16700294331705165196)
XLA Ops:
  7.2 0.0 copy-start
  7.2 0.0 copy-start.11
  7.2 0.0 all-reduce.3.cloned.1.call-start
  7.3 0.0 copy-start.7
  7.3 0.0 copy-start.8
  7.3 1.7 copy_bitcast_fusion
  9.0 0.0 all-reduce.3.cloned.1.call-update
  9.0 0.0 reduce-scatter.4.cloned.1.call-start
  9.1 1.7 dynamic-slice_bitcast_fusion
  10.8 0.0 reduce-scatter.4.cloned.1.call-update
  10.8 0.0 reduce-scatter.6.cloned.1.call-start
  10.8 0.0 copy-start.2
  10.8 0.7 reduce-scatter.6.cloned.1.call-update
  11.5 0.0 all-gather.4.cloned.1.call-start
  11.6 0.6 dynamic-slice
  12.2 41.8 %all-reduce.3.cloned.1.call-done = bf16[4,2,8,2048]{3,2,0,1:T(8,128)(2,1)} async-done(((bf16[4,2,8,2048]{3,2,0,1:T(8,128)(2,1)}), bf16[4,2,8,2048]{3,2,0,1:T(8,128)(2,1)}) %all-reduce.3.cloned.1.call-update) | async-done | bytes 262160
  54.0 1.5 dynamic-slice_convert_fusion
  55.5 8.6 %all_to_all.28 = f32[1,2,8,2048]{3,2,0,1:T(8,128)S(1)} all-to-all(f32[1,2,8,2048]{3,2,0,1:T(8,128)S(1)} %dynamic-slice_convert_fusion), channel_id=1, replica_groups=mesh['replica'=4,'shard'=16,'tensor'=2] {'tensor'}, dimensions={1} | all-to-all | bytes 262144 | tf_op jit(solution)/shard_map/all_to_all | solution.py:72
  64.1 0.7 fusion.15
  64.8 7.5 %all_to_all.29 = bf16[8,2,2048]{2,0,1:T(8,128)(2,1)} all-to-all(bf16[8,2,2048]{2,0,1:T(8,128)(2,1)S(1)} %bitcast.53), channel_id=1, replica_groups=mesh['replica'=4,'shard'=16,'tensor'=2] {'tensor'}, dimensions={1} | all-to-all | bytes 131072 | tf_op jit(solution)/shard_map/all_to_all | solution.py:92
  72.4 0.0 all-gather.4.cloned.1.call-update
  72.4 0.0 all-gather.6.cloned.1.call-start
  72.4 6.0 %reduce-scatter.4.cloned.1.call-done = bf16[1,32,1024]{2,1,0:T(8,128)(2,1)} async-done(((bf16[4,32,1024]{2,1,0:T(8,128)(2,1)}), bf16[1,32,1024]{2,1,0:T(8,128)(2,1)}) %reduce-scatter.4.cloned.1.call-update) | async-done | bytes 65552 | tf_op jit(solution)/shard_map/reduce_scatter | solution.py:65
  78.4 0.0 copy-done.6
  78.4 1.6 fusion.14
  80.0 0.0 all-gather.6.cloned.1.call-update
  80.0 32.4 %reduce-scatter.6.cloned.1.call-done = bf16[1,256,1024]{2,1,0:T(8,128)(2,1)} async-done(((bf16[4,256,1024]{2,1,0:T(8,128)(2,1)}), bf16[1,256,1024]{2,1,0:T(8,128)(2,1)}) %reduce-scatter.6.cloned.1.call-update) | async-done | bytes 524304 | tf_op jit(solution)/shard_map/reduce_scatter | solution.py:82
  112.4 2.2 fusion.1
  114.6 0.3 broadcast_in_dim.9
  114.8 0.0 copy-done.4
  114.8 0.0 copy-start.10
  114.8 0.0 copy-start.9
  114.9 2.2 constant_dynamic-update-slice_fusion.3
  117.1 0.0 collective-permute-start
  117.1 16.2 %psum.7 = f32[2,1024]{1,0:T(2,128)S(1)} all-reduce(f32[2,1024]{1,0:T(2,128)S(1)} %bitcast_convert_fusion), channel_id=1, replica_groups=mesh['replica'=4,'shard'=16,'tensor'=2] {'replica'}, use_global_device_ids=true, to_apply=%region_3.4 | all-reduce | flops 2048 | bytes 16384 | tf_op jit(solution)/shard_map/psum | solution.py:77
  133.3 1.4 collective-permute-start.1
  134.7 0.0 collective-permute-done
  134.7 0.1 collective-permute-start.2
  134.8 1.3 fusion.13
  136.1 0.6 fusion.8
  136.8 10.6 %collective-permute-done.1 = bf16[256,1024]{1,0:T(8,128)(2,1)} collective-permute-done((bf16[256,1024]{1,0:T(8,128)(2,1)}, bf16[256,1024]{1,0:T(8,128)(2,1)}, u32[]{:S(2)}, u32[]{:S(2)}) %collective-permute-start.1) | collective-permute-done | bytes 524320 | tf_op jit(solution)/shard_map/ppermute | solution.py:18
  147.4 1.1 constant_dynamic-update-slice_fusion.1
  148.5 0.0 collective-permute-done.2
  148.5 0.0 copy-start.3
  148.6 72.1 %all-gather.4.cloned.1.call-done = bf16[1024,2048]{1,0:T(8,128)(2,1)} async-done(((bf16[16,2048]{1,0:T(8,128)(2,1)}), bf16[1024,2048]{1,0:T(8,128)(2,1)}) %all-gather.4.cloned.1.call-update) | async-done | bytes 4194320 | tf_op jit(solution)/shard_map/all_gather | solution.py:97
  220.7 107.2 %all-gather.6.cloned.1.call-done = bf16[1,2048,1024]{2,1,0:T(8,128)(2,1)} async-done(((bf16[1,32,1024]{2,1,0:T(8,128)(2,1)}), bf16[1,2048,1024]{2,1,0:T(8,128)(2,1)}) %all-gather.6.cloned.1.call-update) | async-done | bytes 4194320 | tf_op jit(solution)/shard_map/all_gather | solution.py:98
  327.9 4.9 %copy.42 = bf16[1024,2048]{1,0:T(8,128)(2,1)} copy(bf16[1024,2048]{1,0:T(8,128)(2,1)} %all-gather.4.cloned.1.call-done) | data formatting | bytes 8388608
  332.8 2.0 copy.43
  (18 shorter events, 0.1 us)
Async XLA Ops:
  7.2 105.2 %copy-start = (f32[1024,64]{0,1:T(8,128)S(1)}, f32[1024,64]{0,1:T(8,128)}, u32[]{:S(2)}) copy-start(f32[1024,64]{0,1:T(8,128)} %param.25) | copy-start | bytes 786436
  7.2 4.4 %copy-start.11 = (u32[128]{0:T(128)S(1)}, u32[128]{0:T(128)}, u32[]{:S(2)}) copy-start(u32[128]{0:T(128)} %constant.87) | copy-start | bytes 1540
  7.2 46.8 %all-reduce.3.cloned.1.call-start = ((), (), s32[]{:S(2)}) async-start(), calls=%async_computation.8 | async-start | bytes 524288
  7.3 56.8 %copy-start.7 = (f32[8,4096]{1,0:T(8,128)S(1)}, f32[8,4096]{1,0:T(8,128)}, u32[]{:S(2)}) copy-start(f32[8,4096]{1,0:T(8,128)} %param.17) | copy-start | bytes 393220
  7.3 56.8 %copy-start.8 = (f32[8,4096]{1,0:T(8,128)S(1)}, f32[8,4096]{1,0:T(8,128)}, u32[]{:S(2)}) copy-start(f32[8,4096]{1,0:T(8,128)} %param.18) | copy-start | bytes 393220
  9.0 69.4 %reduce-scatter.4.cloned.1.call-start = ((), (), s32[]{:S(2)}) async-start(), calls=%async_computation.5 | async-start | bytes 327680 | tf_op jit(solution)/shard_map/reduce_scatter | solution.py:65
  10.8 67.6 %copy-start.5 = (f32[1,32,1024]{2,1,0:T(8,128)S(1)}, f32[1,32,1024]{2,1,0:T(8,128)}, u32[]{:S(2)}) copy-start(f32[1,32,1024]{2,1,0:T(8,128)} %param.19) | copy-start | bytes 393220
  10.8 67.6 %copy-start.6 = (f32[1,32,1024]{2,1,0:T(8,128)S(1)}, f32[1,32,1024]{2,1,0:T(8,128)}, u32[]{:S(2)}) copy-start(f32[1,32,1024]{2,1,0:T(8,128)} %param.20) | copy-start | bytes 393220
  10.8 101.6 %reduce-scatter.6.cloned.1.call-start = ((), (), s32[]{:S(2)}) async-start(), calls=%async_computation.6 | async-start | bytes 2621440 | tf_op jit(solution)/shard_map/reduce_scatter | solution.py:82
  10.8 101.6 %copy-start.2 = (f32[1,256,1024]{2,1,0:T(8,128)S(1)}, f32[1,256,1024]{2,1,0:T(8,128)}, u32[]{:S(2)}) copy-start(f32[1,256,1024]{2,1,0:T(8,128)} %param.21) | copy-start | bytes 3145732
  11.5 209.2 %all-gather.4.cloned.1.call-start = ((), (), s32[]{:S(2)}) async-start(), calls=%async_computation.4 | async-start | bytes 4259840 | tf_op jit(solution)/shard_map/all_gather | solution.py:97
  72.4 255.5 %all-gather.6.cloned.1.call-start = ((), (), s32[]{:S(2)}) async-start(), calls=%async_computation.7 | async-start | bytes 4259840 | tf_op jit(solution)/shard_map/all_gather | solution.py:98
  80.0 34.8 %copy-start.4 = (f32[1,256,64]{1,2,0:T(8,128)S(1)}, f32[1,256,64]{1,2,0:T(8,128)}, u32[]{:S(2)}) copy-start(f32[1,256,64]{1,2,0:T(8,128)} %param.22) | copy-start | bytes 196612
  114.8 2.3 copy-start.10
  114.8 20.0 %copy-start.9 = (f32[2,1024]{1,0:T(2,128)S(1)}, f32[2,1024]{1,0:T(2,128)}, u32[]{:S(2)}) copy-start(f32[2,1024]{1,0:T(2,128)} %param.23) | copy-start | bytes 24580
  117.1 17.6 %collective-permute-start = (bf16[256,1024]{1,0:T(8,128)(2,1)}, bf16[256,1024]{1,0:T(8,128)(2,1)S(1)}, u32[]{:S(2)}, u32[]{:S(2)}) collective-permute-start(bf16[256,1024]{1,0:T(8,128)(2,1)} %get-tuple-element.16), channel_id=1, source_target_pairs={{0,32},{32,64},{64,96},{96,0},{1,33},{33,65},{65,97},{97,1},{2,34}... | collective-permute-start | bytes 1572872 | tf_op jit(solution)/shard_map/ppermute | solution.py:15
  133.3 14.1 %collective-permute-start.1 = (bf16[256,1024]{1,0:T(8,128)(2,1)}, bf16[256,1024]{1,0:T(8,128)(2,1)}, u32[]{:S(2)}, u32[]{:S(2)}) collective-permute-start(bf16[256,1024]{1,0:T(8,128)(2,1)} %get-tuple-element.16), channel_id=1, source_target_pairs={{0,96},{32,0},{64,32},{96,64},{1,97},{33,1},{65,33},{97,65},{2,98}... | collective-permute-start | bytes 1572872 | tf_op jit(solution)/shard_map/ppermute | solution.py:18
  134.7 13.8 %collective-permute-start.2 = (bf16[256,1024]{1,0:T(8,128)(2,1)S(1)}, bf16[256,1024]{1,0:T(8,128)(2,1)S(1)}, u32[]{:S(2)}, u32[]{:S(2)}) collective-permute-start(bf16[256,1024]{1,0:T(8,128)(2,1)S(1)} %collective-permute-done), channel_id=1, source_target_pairs={{0,32},{32,64},{64,96},{96,0},{1,33},{33,65},{65,97},{97,1},{2,34}... | collective-permute-start | bytes 1572872 | tf_op jit(solution)/shard_map/ppermute | solution.py:15
  148.5 184.3 %copy-start.3 = (bf16[1024,1024]{1,0:T(8,128)(2,1)}, bf16[1024,1024]{1,0:T(8,128)(2,1)S(1)}, u32[]{:S(2)}) copy-start(bf16[1024,1024]{1,0:T(8,128)(2,1)S(1)} %constant_dynamic-update-slice_fusion) | copy-start | bytes 6291460
  327.9 4.9 %copy-start.1 = (bf16[1,2048,1024]{2,1,0:T(8,128)(2,1)S(1)}, bf16[1,2048,1024]{2,1,0:T(8,128)(2,1)}, u32[]{:S(2)}) copy-start(bf16[1,2048,1024]{2,1,0:T(8,128)(2,1)} %all-gather.6.cloned.1.call-done) | copy-start | bytes 12582916
Sparse Core Ops, SparseCore 0:
  10.9 42.9 all-reduce.2
  57.0 21.2 reduce-scatter.3
  80.8 31.5 reduce-scatter.5
  114.1 106.5 all-gather.3
  222.9 104.8 all-gather.5
